TPU v7x, 256 devices: a whole 4x4x8 slice. The times are simulated.
256 devices in a mesh: leaf: 64 (over x, z, core), front: 4 (over y).
Axes of the slice: x: 4, y: 4, z: 8, core: 2. Of those that a mesh axis runs over, the one named last changes fastest.
Arguments:
- leaf_update: float32 [65536, 1024], P('leaf'), as said below
- separator_rows_1: float32 [16384, 1536], P(('leaf', 'front')), as said below
- remaining_rows_1: float32 [32768, 1536], P(('leaf', 'front'))
- separator_rows_2: float32 [8192, 1536], P(('leaf', 'front')), as said below
- remaining_rows_2: float32 [16384, 1536], P(('leaf', 'front'))
- separator_rows_3: float32 [4096, 1536], P(('leaf', 'front')), as said below
- remaining_rows_3: float32 [8192, 1536], P(('leaf', 'front'))
- child_map_1: int32 [64, 8], replicated, may hold values from 0 to 11, as said below
- child_map_2: int32 [32, 8], replicated, may hold values from 0 to 11, as said below
- child_map_3: int32 [16, 8], replicated, may hold values from 0 to 11, as said below
Outputs:
- pivot_factor_1: float32 [16384, 512], P(('leaf', 'front'))
- below_factor_1: float32 [32768, 512], P(('leaf', 'front'))
- pivot_factor_2: float32 [8192, 512], P(('leaf', 'front'))
- below_factor_2: float32 [16384, 512], P(('leaf', 'front'))
- pivot_factor_3: float32 [4096, 512], P(('leaf', 'front'))
- below_factor_3: float32 [8192, 512], P(('leaf', 'front'))
Inputs may be any that keep to these rules, and one draw needn't show every extreme that they name: `child_map_1`: each row lists 8 distinct parent tiles in increasing order, the last one always 12 - 1. `child_map_2`: each row lists 8 distinct parent tiles in increasing order, the last one always 12 - 1. `child_map_3`: each row lists 8 distinct parent tiles in increasing order, the last one always 12 - 1. `leaf_update`: each block is symmetric positive definite, diagonal between 0.5 and 2, off-diagonal entries of magnitude about 0.008, smallest eigenvalue about 0.1 or more. Each front, separator_rows_1 above remaining_rows_1, is symmetric positive definite, diagonal between 2 and 4, off-diagonal entries of magnitude about 0.03, smallest eigenvalue about 0.35 or more. Each front, separator_rows_2 above remaining_rows_2, is symmetric positive definite, diagonal between 2 and 4, off-diagonal entries of magnitude about 0.03, smallest eigenvalue about 0.35 or more. Each front, separator_rows_3 above remaining_rows_3, is symmetric positive definite, diagonal between 2 and 4, off-diagonal entries of magnitude about 0.03, smallest eigenvalue about 0.35 or more.
All inputs are finite; a program needn't handle non-finite values.
Results may differ from a plain program's by a relative error of at most 0.0003.
Values sent between devices are 32-bit elements; how exact they have to be, the bound alone decides.
No kernel may reach another device: no remote copies, remote signals or barrier semaphores. Data moves between devices by JAX's collectives and lax.ppermute only.
A program may use at most 128 MiB of HBM per device.

v0:
```python
import jax
import jax.numpy as jnp
from jax import lax
from jax.sharding import PartitionSpec as P

TILE = 128
SEP = 512
UPD = 1024
NF = 1536
NT = 12
UT = 8


def from_partner(block, axis, stride):
    count = lax.axis_size(axis)
    route = []
    for low in range(count):
        high = low | 1 << stride
        if high != low and high < count:
            route += [(low, high), (high, low)]
    return lax.ppermute(block, axis, route)


def collect(pieces, depth_count):
    gathered = lax.all_gather(pieces, "front", axis=0, tiled=True)
    leaf_place = lax.axis_index("leaf")
    for bit_number in range(depth_count):
        partner = from_partner(gathered, "leaf", bit_number)
        on_high = leaf_place >> bit_number & 1 == 1
        gathered = jnp.where(
            on_high,
            jnp.concatenate([partner, gathered], axis=0),
            jnp.concatenate([gathered, partner], axis=0),
        )
    return gathered


def owned_rows(position, group_count):
    sep_count = SEP // group_count
    upd_count = UPD // group_count
    sep_index = position * sep_count + jnp.arange(sep_count, dtype=jnp.int32)
    upd_index = SEP + position * upd_count + jnp.arange(upd_count, dtype=jnp.int32)
    return jnp.concatenate([sep_index, upd_index])


def locate(tile_map, targets):
    tile_of = targets // TILE
    offset = targets % TILE
    matches = tile_map[None, :] == tile_of[:, None]
    present = jnp.any(matches, axis=1)
    slot_ids = jnp.arange(tile_map.shape[0], dtype=jnp.int32)
    source = jnp.sum(jnp.where(matches, slot_ids[None, :], 0), axis=1)
    return (source * TILE + offset, present)


def select_rows(full_update, tile_map, targets):
    source, present = locate(tile_map, targets)
    return jnp.where(present[:, None], jnp.take(full_update, source, axis=0), 0.0)


def expand_columns(row_block, tile_map):
    placing = (tile_map[:, None] == jnp.arange(NT, dtype=jnp.int32)[None, :]).astype(jnp.float32)
    tiled = row_block.reshape(row_block.shape[0], UT, TILE)
    placed = jnp.einsum("rut,un->rnt", tiled, placing, precision=lax.Precision.HIGHEST)
    return placed.reshape(row_block.shape[0], NF)


def body(
    leaf_update,
    separator_rows_1,
    remaining_rows_1,
    separator_rows_2,
    remaining_rows_2,
    separator_rows_3,
    remaining_rows_3,
    child_map_1,
    child_map_2,
    child_map_3,
):
    leaf_place = lax.axis_index("leaf")
    front_place = lax.axis_index("front")
    front_count = lax.axis_size("front")
    child_full = leaf_update
    sections = (
        (separator_rows_1, remaining_rows_1, child_map_1),
        (separator_rows_2, remaining_rows_2, child_map_2),
        (separator_rows_3, remaining_rows_3, child_map_3),
    )
    results = []
    for level_number in range(1, 4):
        sep_part, upd_part, child_maps = sections[level_number - 1]
        group_count = front_count * 2**level_number
        sep_count = SEP // group_count
        upd_count = UPD // group_count
        pair_bit = level_number - 1
        child_front = leaf_place >> pair_bit
        sibling_front = child_front ^ 1
        position = leaf_place % 2**level_number * front_count + front_place
        own_map = lax.dynamic_index_in_dim(child_maps, child_front, 0, keepdims=False)
        targets = owned_rows(position, group_count)
        sibling_map = lax.dynamic_index_in_dim(child_maps, sibling_front, 0, keepdims=False)
        sibling_full = from_partner(child_full, "leaf", pair_bit)
        sibling_block = select_rows(sibling_full, sibling_map, targets)
        own_term = expand_columns(select_rows(child_full, own_map, targets), own_map)
        sibling_term = expand_columns(sibling_block, sibling_map)
        is_odd = child_front & 1 == 1
        earlier_term = jnp.where(is_odd, sibling_term, own_term)
        later_term = jnp.where(is_odd, own_term, sibling_term)
        front_rows = jnp.concatenate([sep_part, upd_part], axis=0) + earlier_term + later_term
        panel_all = collect(front_rows[:, :SEP], level_number)
        blocks = panel_all.reshape(group_count, sep_count + upd_count, SEP)
        pivot_block = blocks[:, :sep_count].reshape(SEP, SEP)
        lower_block = blocks[:, sep_count:].reshape(UPD, SEP)
        diag_factor = jnp.linalg.cholesky(pivot_block)
        solved_all = lax.linalg.triangular_solve(
            diag_factor, lower_block, left_side=False, lower=True, transpose_a=True
        )
        solved_own = lax.dynamic_slice_in_dim(solved_all, position * upd_count, upd_count, 0)
        results.append(lax.dynamic_slice_in_dim(diag_factor, position * sep_count, sep_count, 0))
        results.append(solved_own)
        if level_number < 3:
            update_own = front_rows[sep_count:, SEP:] - jnp.dot(
                solved_own, solved_all.T, precision=lax.Precision.HIGHEST
            )
            child_full = collect(update_own, level_number)
    return (results[0], results[1], results[2], results[3], results[4], results[5])


def solution(mesh):
    in_specs = (
        P("leaf", None),
        P(("leaf", "front"), None),
        P(("leaf", "front"), None),
        P(("leaf", "front"), None),
        P(("leaf", "front"), None),
        P(("leaf", "front"), None),
        P(("leaf", "front"), None),
        P(),
        P(),
        P(),
    )
    out_specs = (
        P(("leaf", "front"), None),
        P(("leaf", "front"), None),
        P(("leaf", "front"), None),
        P(("leaf", "front"), None),
        P(("leaf", "front"), None),
        P(("leaf", "front"), None),
    )
    return jax.shard_map(body, mesh=mesh, in_specs=in_specs, out_specs=out_specs, check_vma=False)
```

profile of v0, /device:TPU:1, one launch (start us, length us, event | category | flops | bytes accessed | tf_op | source)
XLA Modules:
  0.0 1112.1 jit_solution(10254888534688105837)
XLA Ops:
  7.2 3.3 collective-permute-start
  11.8 3.5 gather_fusion.1
  17.7 3.5 gather_fusion
  25.7 30.1 %all-gather.4.cloned.1.call-done = f32[768,512]{1,0:T(8,128)} async-done(((f32[192,512]{1,0:T(8,128)}), f32[768,512]{1,0:T(8,128)}) %all-gather.4.cloned.1.call-update) | async-done | bytes 1572880 | tf_op jit(solution)/shard_map/all_gather | solution.py:25
  57.0 3.2 collective-permute-done.1
  60.3 2.5 maximum_select_fusion.2
  66.7 11.7 %cholesky.374 = f32[128,128]{1,0:T(8,128)S(1)} custom-call(f32[128,128]{1,0:T(8,128)S(1)} %cholesky.586), custom_call_target="Cholesky" | custom-call | tf_op jit(solution)/shard_map/jit(cholesky)/cholesky | solution.py:114
  78.6 9.8 custom-call.31
  90.9 11.7 %cholesky.393 = f32[128,128]{1,0:T(8,128)S(1)} custom-call(f32[128,128]{1,0:T(8,128)S(1)} %cholesky.590), custom_call_target="Cholesky" | custom-call | tf_op jit(solution)/shard_map/jit(cholesky)/cholesky | solution.py:114
  102.7 10.0 custom-call.32
  114.2 11.7 %cholesky.414 = f32[128,128]{1,0:T(8,128)S(1)} custom-call(f32[128,128]{1,0:T(8,128)S(1)} %cholesky.595), custom_call_target="Cholesky" | custom-call | tf_op jit(solution)/shard_map/jit(cholesky)/cholesky | solution.py:114
  126.0 9.8 custom-call.33
  137.2 12.1 %cholesky.431 = f32[128,128]{1,0:T(8,128)S(1)} custom-call(f32[128,128]{1,0:T(8,128)S(1)} %convolution_subtract_fusion.10), custom_call_target="Cholesky" | custom-call | tf_op jit(solution)/shard_map/jit(cholesky)/cholesky | solution.py:114
  156.1 11.6 %while.6 = (s32[]{:T(128)}, f32[512,512]{1,0:T(8,128)}, s32[4,2]{0,1:T(2,128)S(1)}, f32[4,128,128]{2,1,0:T(8,128)S(1)}, s32[]{:T(128)}) while((s32[]{:T(128)}, f32[512,512]{1,0:T(8,128)}, s32[4,2]{0,1:T(2,128)S(1)}, f32[4,128,128]{2,1,0:T(8,128)S(1)}, s32[]{:T(128)}) %tuple.112), condition=%wide.while_cond, body=%wide.while_body.sunk | while | flops 2 | bytes 131189 | solution.py:115
  156.7 2.3 bitcast_dynamic-update-slice_fusion.6
  159.6 2.3 bitcast_dynamic-update-slice_fusion.6
  162.5 2.3 bitcast_dynamic-update-slice_fusion.6
  167.7 39.3 %custom-call.34 = f32[4,128,128]{1,2,0:T(8,128)S(1)} custom-call(f32[4,128,128]{2,1,0:T(8,128)S(1)} %get-tuple-element.31), custom_call_target="InvertDiagBlocksLowerTriangular" | custom-call | tf_op jit(solution)/shard_map/triangular_solve/custom-call.3 | solution.py:115
  210.2 2.7 fusion.18
  213.6 3.7 fusion
  218.9 3.2 convolution_subtract_fusion
  222.2 33.3 %all-gather.6.cloned.1.call-done = f32[512,1024]{1,0:T(8,128)} async-done(((f32[128,1024]{1,0:T(8,128)}), f32[512,1024]{1,0:T(8,128)}) %all-gather.6.cloned.1.call-update) | async-done | bytes 2097168 | tf_op jit(solution)/shard_map/all_gather | solution.py:25
  256.3 4.0 collective-permute-done.2
  260.3 5.1 maximum_select_fusion
  267.0 3.1 gather_fusion.3
  270.9 86.6 %collective-permute-done.3 = f32[1024,1024]{1,0:T(8,128)} collective-permute-done((f32[1024,1024]{1,0:T(8,128)}, f32[1024,1024]{1,0:T(8,128)}, u32[]{:S(2)}, u32[]{:S(2)}) %collective-permute-start.3) | collective-permute-done | bytes 4194336 | tf_op jit(solution)/shard_map/ppermute | solution.py:21
  357.5 3.1 gather_fusion.2
  362.2 10.7 all_gather.17
  372.9 4.8 collective-permute-start.4
  381.1 34.3 %collective-permute-done.5 = f32[768,512]{1,0:T(8,128)S(1)} collective-permute-done((f32[768,512]{1,0:T(8,128)S(1)}, f32[768,512]{1,0:T(8,128)S(1)}, u32[]{:S(2)}, u32[]{:S(2)}) %collective-permute-start.5) | collective-permute-done | bytes 1572896 | tf_op jit(solution)/shard_map/ppermute | solution.py:21
  419.8 11.7 %cholesky.446 = f32[128,128]{1,0:T(8,128)S(1)} custom-call(f32[128,128]{1,0:T(8,128)S(1)} %cholesky.599), custom_call_target="Cholesky" | custom-call | tf_op jit(solution)/shard_map/jit(cholesky)/cholesky | solution.py:114
  431.6 9.8 custom-call.35
  444.0 11.7 %cholesky.465 = f32[128,128]{1,0:T(8,128)S(1)} custom-call(f32[128,128]{1,0:T(8,128)S(1)} %cholesky.603), custom_call_target="Cholesky" | custom-call | tf_op jit(solution)/shard_map/jit(cholesky)/cholesky | solution.py:114
  455.7 10.2 custom-call.36
  467.5 11.7 %cholesky.486 = f32[128,128]{1,0:T(8,128)S(1)} custom-call(f32[128,128]{1,0:T(8,128)S(1)} %cholesky.608), custom_call_target="Cholesky" | custom-call | tf_op jit(solution)/shard_map/jit(cholesky)/cholesky | solution.py:114
  479.2 9.8 custom-call.37
  490.5 11.9 %cholesky.503 = f32[128,128]{1,0:T(8,128)S(1)} custom-call(f32[128,128]{1,0:T(8,128)S(1)} %convolution_subtract_fusion.9), custom_call_target="Cholesky" | custom-call | tf_op jit(solution)/shard_map/jit(cholesky)/cholesky | solution.py:114
  509.1 11.6 %while.7 = (s32[]{:T(128)}, f32[512,512]{1,0:T(8,128)}, s32[4,2]{0,1:T(2,128)S(1)}, f32[4,128,128]{2,1,0:T(8,128)S(1)}, s32[]{:T(128)}) while((s32[]{:T(128)}, f32[512,512]{1,0:T(8,128)}, s32[4,2]{0,1:T(2,128)S(1)}, f32[4,128,128]{2,1,0:T(8,128)S(1)}, s32[]{:T(128)}) %tuple.127), condition=%wide.while_cond.clone, body=%wide.while_body.clone.sunk | while | flops 2 | bytes 131189 | solution.py:115
  520.7 39.3 %custom-call.38 = f32[4,128,128]{1,2,0:T(8,128)S(1)} custom-call(f32[4,128,128]{2,1,0:T(8,128)S(1)} %get-tuple-element.32), custom_call_target="InvertDiagBlocksLowerTriangular" | custom-call | tf_op jit(solution)/shard_map/triangular_solve/custom-call.3 | solution.py:115
  563.2 2.7 fusion.22
  566.6 3.7 fusion.6
  571.3 3.1 convolution_subtract_fusion.1
  574.4 26.1 %all-gather.8.cloned.1.call-done = f32[256,1024]{1,0:T(8,128)} async-done(((f32[64,1024]{1,0:T(8,128)}), f32[256,1024]{1,0:T(8,128)}) %all-gather.8.cloned.1.call-update) | async-done | bytes 1048592 | tf_op jit(solution)/shard_map/all_gather | solution.py:25
  602.5 2.5 collective-permute-done.6
  608.2 45.6 %collective-permute-done.7 = f32[512,1024]{1,0:T(8,128)S(1)} collective-permute-done((f32[512,1024]{1,0:T(8,128)S(1)}, f32[512,1024]{1,0:T(8,128)S(1)}, u32[]{:S(2)}, u32[]{:S(2)}) %collective-permute-start.7) | collective-permute-done | bytes 2097184 | tf_op jit(solution)/shard_map/ppermute | solution.py:21
  653.7 2.4 maximum_select_fusion.1
  658.9 2.9 gather_fusion.5
  662.4 176.2 %collective-permute-done.8 = f32[1024,1024]{1,0:T(8,128)} collective-permute-done((f32[1024,1024]{1,0:T(8,128)}, f32[1024,1024]{1,0:T(8,128)}, u32[]{:S(2)}, u32[]{:S(2)}) %collective-permute-start.8) | collective-permute-done | bytes 4194336 | tf_op jit(solution)/shard_map/ppermute | solution.py:21
  838.6 2.9 gather_fusion.4
  842.6 10.9 all_gather.19
  853.5 3.5 collective-permute-start.9
  858.5 18.7 %collective-permute-done.10 = f32[384,512]{1,0:T(8,128)S(1)} collective-permute-done((f32[384,512]{1,0:T(8,128)S(1)}, f32[384,512]{1,0:T(8,128)S(1)}, u32[]{:S(2)}, u32[]{:S(2)}) %collective-permute-start.10) | collective-permute-done | bytes 786464 | tf_op jit(solution)/shard_map/ppermute | solution.py:21
  885.1 62.8 %collective-permute-done.11 = f32[768,512]{1,0:T(8,128)S(1)} collective-permute-done((f32[768,512]{1,0:T(8,128)S(1)}, f32[768,512]{1,0:T(8,128)S(1)}, u32[]{:S(2)}, u32[]{:S(2)}) %collective-permute-start.11) | collective-permute-done | bytes 1572896 | tf_op jit(solution)/shard_map/ppermute | solution.py:21
  952.3 11.7 %cholesky.518 = f32[128,128]{1,0:T(8,128)S(1)} custom-call(f32[128,128]{1,0:T(8,128)S(1)} %cholesky.612), custom_call_target="Cholesky" | custom-call | tf_op jit(solution)/shard_map/jit(cholesky)/cholesky | solution.py:114
  964.2 9.8 custom-call.39
  976.5 11.7 %cholesky.537 = f32[128,128]{1,0:T(8,128)S(1)} custom-call(f32[128,128]{1,0:T(8,128)S(1)} %cholesky.616), custom_call_target="Cholesky" | custom-call | tf_op jit(solution)/shard_map/jit(cholesky)/cholesky | solution.py:114
  988.2 9.9 custom-call.40
  999.8 11.7 %cholesky.558 = f32[128,128]{1,0:T(8,128)S(1)} custom-call(f32[128,128]{1,0:T(8,128)S(1)} %cholesky.621), custom_call_target="Cholesky" | custom-call | tf_op jit(solution)/shard_map/jit(cholesky)/cholesky | solution.py:114
  1011.5 9.8 custom-call.41
  1022.8 11.9 %cholesky.575 = f32[128,128]{1,0:T(8,128)S(1)} custom-call(f32[128,128]{1,0:T(8,128)S(1)} %convolution_subtract_fusion.8), custom_call_target="Cholesky" | custom-call | tf_op jit(solution)/shard_map/jit(cholesky)/cholesky | solution.py:114
  1041.6 11.5 %while.8 = (s32[]{:T(128)}, f32[512,512]{1,0:T(8,128)}, s32[4,2]{0,1:T(2,128)S(1)}, f32[4,128,128]{2,1,0:T(8,128)S(1)}, s32[]{:T(128)}) while((s32[]{:T(128)}, f32[512,512]{1,0:T(8,128)}, s32[4,2]{0,1:T(2,128)S(1)}, f32[4,128,128]{2,1,0:T(8,128)S(1)}, s32[]{:T(128)}) %tuple.128), condition=%wide.while_cond.clone.1, body=%wide.while_body.clone.1.sunk | while | flops 2 | bytes 131189 | solution.py:115
  1053.0 39.3 %custom-call.42 = f32[4,128,128]{1,2,0:T(8,128)S(1)} custom-call(f32[4,128,128]{2,1,0:T(8,128)S(1)} %get-tuple-element.33), custom_call_target="InvertDiagBlocksLowerTriangular" | custom-call | tf_op jit(solution)/shard_map/triangular_solve/custom-call.3 | solution.py:115
  1095.5 2.7 fusion.26
  1098.8 3.6 fusion.12
  (234 shorter events, 122.8 us)
Async XLA Ops:
  7.2 48.7 %all-gather.4.cloned.1.call-start = ((), (), s32[]{:S(2)}) async-start(), calls=%async_computation | async-start | bytes 1966080 | tf_op jit(solution)/shard_map/all_gather | solution.py:25
  7.2 10.5 collective-permute-start
  21.5 1.1 copy-start.6
  21.5 1.2 copy-start.8
  23.9 1.0 copy-start.3
  25.7 229.8 %all-gather.6.cloned.1.call-start = ((), (), s32[]{:S(2)}) async-start(), calls=%async_computation.1 | async-start | bytes 2621440 | tf_op jit(solution)/shard_map/all_gather | solution.py:25
  55.9 4.4 collective-permute-start.1
  65.7 1.0 copy-start
  218.2 0.7 copy-start.4
  222.1 378.4 %all-gather.8.cloned.1.call-start = ((), (), s32[]{:S(2)}) async-start(), calls=%async_computation.2 | async-start | bytes 1310720 | tf_op jit(solution)/shard_map/all_gather | solution.py:25
  255.5 4.8 collective-permute-start.2
  265.4 92.1 %collective-permute-start.3 = (f32[1024,1024]{1,0:T(8,128)}, f32[1024,1024]{1,0:T(8,128)}, u32[]{:S(2)}, u32[]{:S(2)}) collective-permute-start(f32[1024,1024]{1,0:T(8,128)} %maximum_select_fusion), channel_id=1, source_target_pairs={{0,8},{8,0},{4,12},{12,4},{16,24},{24,16},{20,28},{28,20},{32,40},... | collective-permute-start | bytes 12582920 | tf_op jit(solution)/shard_map/ppermute | solution.py:21
  360.6 1.0 copy-start.7
  360.6 1.0 copy-start.10
  362.2 15.5 %copy-start.5 = (f32[96,1536]{1,0:T(8,128)}, f32[96,1536]{1,0:T(8,128)S(1)}, u32[]{:S(2)}) copy-start(f32[96,1536]{1,0:T(8,128)S(1)} %bitcast_add_fusion.5) | copy-start | bytes 1769476
  372.9 6.7 collective-permute-start.4
  379.7 35.7 %collective-permute-start.5 = (f32[768,512]{1,0:T(8,128)S(1)}, f32[768,512]{1,0:T(8,128)S(1)}, u32[]{:S(2)}, u32[]{:S(2)}) collective-permute-start(f32[768,512]{1,0:T(8,128)S(1)} %maximum_select_fusion.6), channel_id=1, source_target_pairs={{0,8},{8,0},{4,12},{12,4},{16,24},{24,16},{20,28},{28,20},{32,40},... | collective-permute-start | bytes 4718600 | tf_op jit(solution)/shard_map/ppermute | solution.py:21
  418.8 1.0 copy-start.1
  600.5 4.5 collective-permute-start.6
  606.8 51.6 %copy-start.12 = (s32[16,8]{0,1:T(8,128)S(1)}, s32[16,8]{0,1:T(8,128)}, u32[]{:S(2)}) copy-start(s32[16,8]{0,1:T(8,128)} %param.28) | copy-start | bytes 1540
  606.8 46.9 %collective-permute-start.7 = (f32[512,1024]{1,0:T(8,128)S(1)}, f32[512,1024]{1,0:T(8,128)S(1)}, u32[]{:S(2)}, u32[]{:S(2)}) collective-permute-start(f32[512,1024]{1,0:T(8,128)S(1)} %maximum_select_fusion.5), channel_id=1, source_target_pairs={{0,8},{8,0},{4,12},{12,4},{16,24},{24,16},{20,28},{28,20},{32,40},... | collective-permute-start | bytes 6291464 | tf_op jit(solution)/shard_map/ppermute | solution.py:21
  656.1 182.5 %collective-permute-start.8 = (f32[1024,1024]{1,0:T(8,128)}, f32[1024,1024]{1,0:T(8,128)}, u32[]{:S(2)}, u32[]{:S(2)}) collective-permute-start(f32[1024,1024]{1,0:T(8,128)} %maximum_select_fusion.1), channel_id=1, source_target_pairs={{0,16},{16,0},{4,20},{20,4},{8,24},{24,8},{12,28},{28,12},{32,48},... | collective-permute-start | bytes 12582920 | tf_op jit(solution)/shard_map/ppermute | solution.py:21
  841.6 0.9 copy-start.9
  841.6 1.0 copy-start.11
  853.5 4.9 collective-permute-start.9
  858.4 18.8 %collective-permute-start.10 = (f32[384,512]{1,0:T(8,128)S(1)}, f32[384,512]{1,0:T(8,128)S(1)}, u32[]{:S(2)}, u32[]{:S(2)}) collective-permute-start(f32[384,512]{1,0:T(8,128)S(1)} %maximum_select_fusion.8), channel_id=1, source_target_pairs={{0,8},{8,0},{4,12},{12,4},{16,24},{24,16},{20,28},{28,20},{32,40},... | collective-permute-start | bytes 2359304 | tf_op jit(solution)/shard_map/ppermute | solution.py:21
  877.5 70.5 %collective-permute-start.11 = (f32[768,512]{1,0:T(8,128)S(1)}, f32[768,512]{1,0:T(8,128)S(1)}, u32[]{:S(2)}, u32[]{:S(2)}) collective-permute-start(f32[768,512]{1,0:T(8,128)S(1)} %maximum_select_fusion.7), channel_id=1, source_target_pairs={{0,16},{16,0},{4,20},{20,4},{8,24},{24,8},{12,28},{28,12},{32,48},... | collective-permute-start | bytes 4718600 | tf_op jit(solution)/shard_map/ppermute | solution.py:21
  951.3 1.0 copy-start.2
Sparse Core Ops, SparseCore 0:
  25.8 30.0 all-gather.3
  222.2 33.1 all-gather.5
  574.6 25.8 all-gather.7
where the time goes:
time: 1120 us; the launch traced here: 1110 us
  waiting for transfers between devices  528 us (47%)
  other arithmetic  382 us (34%)
  local copies, waits for them, and re-layouts  74.5 us (7%)
  matrix products  59 us (5%)
  starting transfers between devices  24.1 us (2%)
  between operations  22.8 us (2%)
  blocking collectives  21.5 us (2%)
    ppermute x12, waiting for transfers between devices, from_partner(): return lax.ppermute(block, axis, route)  438 us
    another operation x45, other arithmetic, body(): diag_factor = jnp.linalg.cholesky(pivot_block)  238 us
    another operation x10, other arithmetic, body(): lax.linalg.triangular_solve(diag_factor, lower_block, left_side=False, lo...  123 us
    all_gather x3, waiting for transfers between devices, collect(): gathered = lax.all_gather(pieces, 'front', axis=0, tiled=True)  89.5 us
    another operation x40, local copies, waits for them, and re-layouts, body(): lax.linalg.triangular_solve(diag_factor, lower_block, left_side=False, lo...  34.4 us
    another operation x21, matrix products, body(): lax.linalg.triangular_solve(diag_factor, lower_block, left_side=False, lo...  32.4 us
    ppermute x12, starting transfers between devices, from_partner(): return lax.ppermute(block, axis, route)  24 us
  transfers between devices with their start and end apart: 15, of which 15 were waited for; matrix products, arithmetic and copies ran while one was open for 2% of the time, Pallas kernels for 0%

commit v1 on v0

--- a/solution.py
+++ b/solution.py
@@ -11,6 +11,12 @@
 UT = 8
 
 
+def joined_along(tiles, dim):
+    shape = list(tiles.shape[1:])
+    shape[dim] *= tiles.shape[0]
+    return jnp.moveaxis(tiles, 0, dim).reshape(shape)
+
+
 def from_partner(block, axis, stride):
     count = lax.axis_size(axis)
     route = []
@@ -22,7 +28,19 @@
 
 
 def collect(pieces, depth_count):
-    gathered = lax.all_gather(pieces, "front", axis=0, tiled=True)
+    peers = lax.axis_size("front")
+    pairs = [(i, (i + 1) % peers) for i in range(peers)]
+    back = [(b, a) for a, b in pairs]
+    lower, upper = ([], [])
+    for step in range(peers - 1):
+        if step % 2 == 0:
+            lower.append(lax.ppermute(lower[-1] if lower else pieces, "front", pairs))
+        else:
+            upper.append(lax.ppermute(upper[-1] if upper else pieces, "front", back))
+    parts = jnp.stack([*lower[::-1], pieces, *upper])
+    shift = lax.axis_index("front") - len(lower)
+    parts = parts[(jnp.arange(peers) - shift) % peers]
+    gathered = joined_along(parts, 0)
     leaf_place = lax.axis_index("leaf")
     for bit_number in range(depth_count):
         partner = from_partner(gathered, "leaf", bit_number)

time: 1120 us -> 1090 us (0.973)
  blocking collectives: 21.5 us -> 0 us
  between operations: 22.8 us -> 10 us
  starting transfers between devices: 24.1 us -> 36.5 us
  waiting for transfers between devices: 528 us -> 516 us
    all_gather x3 -> x0, waiting for transfers between devices: 89.5 us -> none  [collect(): gathered = lax.all_gather(pieces, 'front', axis=0, tiled=True)]
    ppermute x0 -> x15, waiting for transfers between devices: none -> 72.7 us  [the longest x10 72.7 us: collect(): lower.append(lax.ppermute(lower[-1] if lower else pieces, 'front', pairs))]
    all_gather x2 -> x0, blocking collectives: 21.5 us -> none  [collect(): gathered = lax.all_gather(pieces, 'front', axis=0, tiled=True)]
    ppermute x0 -> x15, starting transfers between devices: none -> 14.4 us  [the longest x5 13.3 us: collect(): upper.append(lax.ppermute(upper[-1] if upper else pieces, 'front', back))]
  transfers between devices with their start and end apart: 15 -> 27, of which waited for: 15 -> 22; matrix products, arithmetic and copies ran while one was open for 2% -> 2% of each run, Pallas kernels for 0% -> 0%
where the time goes in v1:
time: 1090 us; the launch traced here: 1080 us
  waiting for transfers between devices  516 us (47%)
  other arithmetic  379 us (35%)
  local copies, waits for them, and re-layouts  77.6 us (7%)
  matrix products  57.6 us (5%)
  starting transfers between devices  36.5 us (3%)
    ppermute x12, waiting for transfers between devices, from_partner(): return lax.ppermute(block, axis, route)  443 us
    another operation x45, other arithmetic, body(): diag_factor = jnp.linalg.cholesky(pivot_block)  238 us
    another operation x10, other arithmetic, body(): lax.linalg.triangular_solve(diag_factor, lower_block, left_side=False, lo...  123 us
    ppermute x10, waiting for transfers between devices, collect(): lower.append(lax.ppermute(lower[-1] if lower else pieces, 'front', pairs))  72.7 us
    another operation x40, local copies, waits for them, and re-layouts, body(): lax.linalg.triangular_solve(diag_factor, lower_block, left_side=False, lo...  34.4 us
    another operation x21, matrix products, body(): lax.linalg.triangular_solve(diag_factor, lower_block, left_side=False, lo...  32.4 us
    ppermute x12, starting transfers between devices, from_partner(): return lax.ppermute(block, axis, route)  22.2 us
  transfers between devices with their start and end apart: 27, of which 22 were waited for; matrix products, arithmetic and copies ran while one was open for 2% of the time, Pallas kernels for 0%

profile of v1, /device:TPU:1, one launch (start us, length us, event | category | flops | bytes accessed | tf_op | source)
XLA Modules:
  0.0 1076.9 jit_solution(3396033934330308224)
XLA Ops:
  0.6 3.3 collective-permute-start
  5.2 3.5 gather_fusion.6
  11.1 3.5 gather_fusion.5
  18.5 2.7 collective-permute-start.3
  21.2 8.9 collective-permute-done.1
  30.1 10.6 collective-permute-done.2
  43.9 3.0 collective-permute-done.4
  51.3 11.7 %cholesky.374 = f32[128,128]{1,0:T(8,128)S(1)} custom-call(f32[128,128]{1,0:T(8,128)S(1)} %cholesky.586), custom_call_target="Cholesky" | custom-call | tf_op jit(solution)/shard_map/jit(cholesky)/cholesky | solution.py:132
  63.2 9.8 custom-call.31
  75.5 11.7 %cholesky.393 = f32[128,128]{1,0:T(8,128)S(1)} custom-call(f32[128,128]{1,0:T(8,128)S(1)} %cholesky.590), custom_call_target="Cholesky" | custom-call | tf_op jit(solution)/shard_map/jit(cholesky)/cholesky | solution.py:132
  87.3 10.2 custom-call.32
  99.1 11.7 %cholesky.414 = f32[128,128]{1,0:T(8,128)S(1)} custom-call(f32[128,128]{1,0:T(8,128)S(1)} %cholesky.595), custom_call_target="Cholesky" | custom-call | tf_op jit(solution)/shard_map/jit(cholesky)/cholesky | solution.py:132
  110.8 9.8 custom-call.33
  122.1 11.7 %cholesky.431 = f32[128,128]{1,0:T(8,128)S(1)} custom-call(f32[128,128]{1,0:T(8,128)S(1)} %convolution_subtract_fusion.10), custom_call_target="Cholesky" | custom-call | tf_op jit(solution)/shard_map/jit(cholesky)/cholesky | solution.py:132
  140.7 11.7 %while.6 = (s32[]{:T(128)}, f32[512,512]{1,0:T(8,128)}, s32[4,2]{0,1:T(2,128)S(1)}, f32[4,128,128]{2,1,0:T(8,128)S(1)}, s32[]{:T(128)}) while((s32[]{:T(128)}, f32[512,512]{1,0:T(8,128)}, s32[4,2]{0,1:T(2,128)S(1)}, f32[4,128,128]{2,1,0:T(8,128)S(1)}, s32[]{:T(128)}) %tuple.114), condition=%wide.while_cond, body=%wide.while_body.sunk | while | flops 2 | bytes 131189 | solution.py:133
  152.4 39.3 %custom-call.34 = f32[4,128,128]{1,2,0:T(8,128)S(1)} custom-call(f32[4,128,128]{2,1,0:T(8,128)S(1)} %get-tuple-element.31), custom_call_target="InvertDiagBlocksLowerTriangular" | custom-call | tf_op jit(solution)/shard_map/triangular_solve/custom-call.3 | solution.py:133
  194.9 2.7 fusion.18
  198.3 3.7 fusion
  205.7 2.7 collective-permute-start.7
  208.4 11.7 %collective-permute-done.5 = f32[128,1024]{1,0:T(8,128)S(1)} collective-permute-done((f32[128,1024]{1,0:T(8,128)S(1)}, f32[128,1024]{1,0:T(8,128)S(1)}, u32[]{:S(2)}, u32[]{:S(2)}) %collective-permute-start.5) | collective-permute-done | bytes 524320 | tf_op jit(solution)/shard_map/ppermute | solution.py:37
  220.1 13.4 %collective-permute-done.6 = f32[128,1024]{1,0:T(8,128)S(1)} collective-permute-done((f32[128,1024]{1,0:T(8,128)S(1)}, f32[128,1024]{1,0:T(8,128)S(1)}, u32[]{:S(2)}, u32[]{:S(2)}) %collective-permute-start.6) | collective-permute-done | bytes 524320 | tf_op jit(solution)/shard_map/ppermute | solution.py:37
  237.8 4.0 collective-permute-done.8
  241.8 5.1 maximum_select_fusion
  247.3 3.1 gather_fusion.8
  251.2 87.8 %collective-permute-done.9 = f32[1024,1024]{1,0:T(8,128)} collective-permute-done((f32[1024,1024]{1,0:T(8,128)}, f32[1024,1024]{1,0:T(8,128)}, u32[]{:S(2)}, u32[]{:S(2)}) %collective-permute-start.9) | collective-permute-done | bytes 4194336 | tf_op jit(solution)/shard_map/ppermute | solution.py:27
  339.0 3.1 gather_fusion.7
  343.8 2.7 collective-permute-start.12
  346.5 3.7 collective-permute-done.10
  350.2 5.7 collective-permute-done.11
  356.6 3.4 collective-permute-start.13
  362.7 35.6 %collective-permute-done.14 = f32[768,512]{1,0:T(8,128)S(1)} collective-permute-done((f32[768,512]{1,0:T(8,128)S(1)}, f32[768,512]{1,0:T(8,128)S(1)}, u32[]{:S(2)}, u32[]{:S(2)}) %collective-permute-start.14) | collective-permute-done | bytes 1572896 | tf_op jit(solution)/shard_map/ppermute | solution.py:27
  402.6 11.7 %cholesky.446 = f32[128,128]{1,0:T(8,128)S(1)} custom-call(f32[128,128]{1,0:T(8,128)S(1)} %cholesky.599), custom_call_target="Cholesky" | custom-call | tf_op jit(solution)/shard_map/jit(cholesky)/cholesky | solution.py:132
  414.4 9.8 custom-call.35
  426.8 11.7 %cholesky.465 = f32[128,128]{1,0:T(8,128)S(1)} custom-call(f32[128,128]{1,0:T(8,128)S(1)} %cholesky.603), custom_call_target="Cholesky" | custom-call | tf_op jit(solution)/shard_map/jit(cholesky)/cholesky | solution.py:132
  438.5 10.0 custom-call.36
  450.1 11.7 %cholesky.486 = f32[128,128]{1,0:T(8,128)S(1)} custom-call(f32[128,128]{1,0:T(8,128)S(1)} %cholesky.608), custom_call_target="Cholesky" | custom-call | tf_op jit(solution)/shard_map/jit(cholesky)/cholesky | solution.py:132
  461.8 9.8 custom-call.37
  473.1 11.7 %cholesky.503 = f32[128,128]{1,0:T(8,128)S(1)} custom-call(f32[128,128]{1,0:T(8,128)S(1)} %convolution_subtract_fusion.9), custom_call_target="Cholesky" | custom-call | tf_op jit(solution)/shard_map/jit(cholesky)/cholesky | solution.py:132
  491.6 11.8 %while.7 = (s32[]{:T(128)}, f32[512,512]{1,0:T(8,128)}, s32[4,2]{0,1:T(2,128)S(1)}, f32[4,128,128]{2,1,0:T(8,128)S(1)}, s32[]{:T(128)}) while((s32[]{:T(128)}, f32[512,512]{1,0:T(8,128)}, s32[4,2]{0,1:T(2,128)S(1)}, f32[4,128,128]{2,1,0:T(8,128)S(1)}, s32[]{:T(128)}) %tuple.123), condition=%wide.while_cond.clone, body=%wide.while_body.clone.sunk | while | flops 2 | bytes 131189 | solution.py:133
  503.3 39.3 %custom-call.38 = f32[4,128,128]{1,2,0:T(8,128)S(1)} custom-call(f32[4,128,128]{2,1,0:T(8,128)S(1)} %get-tuple-element.32), custom_call_target="InvertDiagBlocksLowerTriangular" | custom-call | tf_op jit(solution)/shard_map/triangular_solve/custom-call.3 | solution.py:133
  545.8 2.7 fusion.22
  549.2 3.7 fusion.6
  559.5 5.1 collective-permute-done.15
  564.6 6.9 collective-permute-done.16
  572.3 3.1 collective-permute-start.18
  578.1 46.8 %collective-permute-done.19 = f32[512,1024]{1,0:T(8,128)S(1)} collective-permute-done((f32[512,1024]{1,0:T(8,128)S(1)}, f32[512,1024]{1,0:T(8,128)S(1)}, u32[]{:S(2)}, u32[]{:S(2)}) %collective-permute-start.19) | collective-permute-done | bytes 2097184 | tf_op jit(solution)/shard_map/ppermute | solution.py:27
  629.5 2.9 gather_fusion.10
  633.0 177.5 %collective-permute-done.20 = f32[1024,1024]{1,0:T(8,128)} collective-permute-done((f32[1024,1024]{1,0:T(8,128)}, f32[1024,1024]{1,0:T(8,128)}, u32[]{:S(2)}, u32[]{:S(2)}) %collective-permute-start.20) | collective-permute-done | bytes 4194336 | tf_op jit(solution)/shard_map/ppermute | solution.py:27
  810.4 2.9 gather_fusion.9
  819.1 4.7 collective-permute-done.22
  824.4 3.3 collective-permute-start.24
  829.2 18.7 %collective-permute-done.25 = f32[384,512]{1,0:T(8,128)S(1)} collective-permute-done((f32[384,512]{1,0:T(8,128)S(1)}, f32[384,512]{1,0:T(8,128)S(1)}, u32[]{:S(2)}, u32[]{:S(2)}) %collective-permute-start.25) | collective-permute-done | bytes 786464 | tf_op jit(solution)/shard_map/ppermute | solution.py:27
  855.8 63.2 %collective-permute-done.26 = f32[768,512]{1,0:T(8,128)S(1)} collective-permute-done((f32[768,512]{1,0:T(8,128)S(1)}, f32[768,512]{1,0:T(8,128)S(1)}, u32[]{:S(2)}, u32[]{:S(2)}) %collective-permute-start.26) | collective-permute-done | bytes 1572896 | tf_op jit(solution)/shard_map/ppermute | solution.py:27
  923.3 11.7 %cholesky.518 = f32[128,128]{1,0:T(8,128)S(1)} custom-call(f32[128,128]{1,0:T(8,128)S(1)} %cholesky.612), custom_call_target="Cholesky" | custom-call | tf_op jit(solution)/shard_map/jit(cholesky)/cholesky | solution.py:132
  935.2 9.8 custom-call.39
  947.5 11.7 %cholesky.537 = f32[128,128]{1,0:T(8,128)S(1)} custom-call(f32[128,128]{1,0:T(8,128)S(1)} %cholesky.616), custom_call_target="Cholesky" | custom-call | tf_op jit(solution)/shard_map/jit(cholesky)/cholesky | solution.py:132
  959.3 10.0 custom-call.40
  970.8 11.7 %cholesky.558 = f32[128,128]{1,0:T(8,128)S(1)} custom-call(f32[128,128]{1,0:T(8,128)S(1)} %cholesky.621), custom_call_target="Cholesky" | custom-call | tf_op jit(solution)/shard_map/jit(cholesky)/cholesky | solution.py:132
  982.6 9.8 custom-call.41
  993.8 12.0 %cholesky.575 = f32[128,128]{1,0:T(8,128)S(1)} custom-call(f32[128,128]{1,0:T(8,128)S(1)} %convolution_subtract_fusion.8), custom_call_target="Cholesky" | custom-call | tf_op jit(solution)/shard_map/jit(cholesky)/cholesky | solution.py:132
  1012.7 11.5 %while.8 = (s32[]{:T(128)}, f32[512,512]{1,0:T(8,128)}, s32[4,2]{0,1:T(2,128)S(1)}, f32[4,128,128]{2,1,0:T(8,128)S(1)}, s32[]{:T(128)}) while((s32[]{:T(128)}, f32[512,512]{1,0:T(8,128)}, s32[4,2]{0,1:T(2,128)S(1)}, f32[4,128,128]{2,1,0:T(8,128)S(1)}, s32[]{:T(128)}) %tuple.124), condition=%wide.while_cond.clone.1, body=%wide.while_body.clone.1.sunk | while | flops 2 | bytes 131189 | solution.py:133
  1024.1 39.3 %custom-call.42 = f32[4,128,128]{1,2,0:T(8,128)S(1)} custom-call(f32[4,128,128]{2,1,0:T(8,128)S(1)} %get-tuple-element.33), custom_call_target="InvertDiagBlocksLowerTriangular" | custom-call | tf_op jit(solution)/shard_map/triangular_solve/custom-call.3 | solution.py:133
  1066.6 2.7 fusion.26
  1070.0 3.6 fusion.12
  (265 shorter events, 146.8 us)
Async XLA Ops:
  0.6 10.5 collective-permute-start
  14.9 1.1 copy-start.6
  14.9 1.2 copy-start.8
  17.3 1.0 copy-start.3
  18.4 11.6 %collective-permute-start.1 = (f32[192,512]{1,0:T(8,128)S(1)}, f32[192,512]{1,0:T(8,128)S(1)}, u32[]{:S(2)}, u32[]{:S(2)}) collective-permute-start(f32[192,512]{1,0:T(8,128)S(1)} %get-tuple-element.127), channel_id=1, source_target_pairs={{0,1},{1,2},{2,3},{3,0},{4,5},{5,6},{6,7},{7,4},{8,9},{9,10},{10,1... | collective-permute-start | bytes 1179656 | tf_op jit(solution)/shard_map/ppermute | solution.py:37
  18.5 11.6 %collective-permute-start.3 = (f32[192,512]{1,0:T(8,128)S(1)}, f32[192,512]{1,0:T(8,128)S(1)}, u32[]{:S(2)}, u32[]{:S(2)}) collective-permute-start(f32[192,512]{1,0:T(8,128)S(1)} %get-tuple-element.127), channel_id=1, source_target_pairs={{1,0},{2,1},{3,2},{0,3},{5,4},{6,5},{7,6},{4,7},{9,8},{10,9},{11,1... | collective-permute-start | bytes 1179656 | tf_op jit(solution)/shard_map/ppermute | solution.py:39
  30.0 10.6 collective-permute-start.2
  41.4 5.5 collective-permute-start.4
  50.3 1.0 copy-start
  202.9 30.5 %copy-start.4 = (f32[128,512]{0,1:T(8,128)}, f32[128,512]{0,1:T(8,128)S(1)}, u32[]{:S(2)}) copy-start(f32[128,512]{0,1:T(8,128)S(1)} %constant_dynamic-slice_fusion.10) | copy-start | bytes 786436
  205.4 14.6 %collective-permute-start.5 = (f32[128,1024]{1,0:T(8,128)S(1)}, f32[128,1024]{1,0:T(8,128)S(1)}, u32[]{:S(2)}, u32[]{:S(2)}) collective-permute-start(f32[128,1024]{1,0:T(8,128)S(1)} %convolution_subtract_fusion), channel_id=1, source_target_pairs={{0,1},{1,2},{2,3},{3,0},{4,5},{5,6},{6,7},{7,4},{8,9},{9,10},{10,1... | collective-permute-start | bytes 1572872 | tf_op jit(solution)/shard_map/ppermute | solution.py:37
  205.7 14.3 %collective-permute-start.7 = (f32[128,1024]{1,0:T(8,128)S(1)}, f32[128,1024]{1,0:T(8,128)S(1)}, u32[]{:S(2)}, u32[]{:S(2)}) collective-permute-start(f32[128,1024]{1,0:T(8,128)S(1)} %convolution_subtract_fusion), channel_id=1, source_target_pairs={{1,0},{2,1},{3,2},{0,3},{5,4},{6,5},{7,6},{4,7},{9,8},{10,9},{11,1... | collective-permute-start | bytes 1572872 | tf_op jit(solution)/shard_map/ppermute | solution.py:39
  220.0 13.4 %collective-permute-start.6 = (f32[128,1024]{1,0:T(8,128)S(1)}, f32[128,1024]{1,0:T(8,128)S(1)}, u32[]{:S(2)}, u32[]{:S(2)}) collective-permute-start(f32[128,1024]{1,0:T(8,128)S(1)} %collective-permute-done.5), channel_id=1, source_target_pairs={{0,1},{1,2},{2,3},{3,0},{4,5},{5,6},{6,7},{7,4},{8,9},{9,10},{10,1... | collective-permute-start | bytes 1572872 | tf_op jit(solution)/shard_map/ppermute | solution.py:37
  235.7 6.1 collective-permute-start.8
  246.9 92.1 %collective-permute-start.9 = (f32[1024,1024]{1,0:T(8,128)}, f32[1024,1024]{1,0:T(8,128)}, u32[]{:S(2)}, u32[]{:S(2)}) collective-permute-start(f32[1024,1024]{1,0:T(8,128)} %maximum_select_fusion), channel_id=1, source_target_pairs={{0,8},{8,0},{4,12},{12,4},{16,24},{24,16},{20,28},{28,20},{32,40},... | collective-permute-start | bytes 12582920 | tf_op jit(solution)/shard_map/ppermute | solution.py:27
  342.1 1.0 copy-start.7
  342.2 1.0 copy-start.10
  343.7 12.3 %copy-start.5 = (f32[96,1536]{1,0:T(8,128)}, f32[96,1536]{1,0:T(8,128)S(1)}, u32[]{:S(2)}) copy-start(f32[96,1536]{1,0:T(8,128)S(1)} %bitcast_add_fusion.5) | copy-start | bytes 1769476
  343.8 6.5 collective-permute-start.10
  343.8 6.4 collective-permute-start.12
  350.2 5.7 collective-permute-start.11
  356.6 5.3 collective-permute-start.13
  362.1 36.1 %collective-permute-start.14 = (f32[768,512]{1,0:T(8,128)S(1)}, f32[768,512]{1,0:T(8,128)S(1)}, u32[]{:S(2)}, u32[]{:S(2)}) collective-permute-start(f32[768,512]{1,0:T(8,128)S(1)} %maximum_select_fusion.6), channel_id=1, source_target_pairs={{0,8},{8,0},{4,12},{12,4},{16,24},{24,16},{20,28},{28,20},{32,40},... | collective-permute-start | bytes 4718600 | tf_op jit(solution)/shard_map/ppermute | solution.py:27
  401.6 1.0 copy-start.1
  556.3 8.3 collective-permute-start.15
  556.8 7.8 collective-permute-start.17
  564.6 6.9 collective-permute-start.16
  572.3 5.4 collective-permute-start.18
  577.9 51.0 %copy-start.12 = (s32[16,8]{0,1:T(8,128)S(1)}, s32[16,8]{0,1:T(8,128)}, u32[]{:S(2)}) copy-start(s32[16,8]{0,1:T(8,128)} %param.28) | copy-start | bytes 1540
  577.9 46.9 %collective-permute-start.19 = (f32[512,1024]{1,0:T(8,128)S(1)}, f32[512,1024]{1,0:T(8,128)S(1)}, u32[]{:S(2)}, u32[]{:S(2)}) collective-permute-start(f32[512,1024]{1,0:T(8,128)S(1)} %maximum_select_fusion.5), channel_id=1, source_target_pairs={{0,8},{8,0},{4,12},{12,4},{16,24},{24,16},{20,28},{28,20},{32,40},... | collective-permute-start | bytes 6291464 | tf_op jit(solution)/shard_map/ppermute | solution.py:27
  627.2 183.2 %collective-permute-start.20 = (f32[1024,1024]{1,0:T(8,128)}, f32[1024,1024]{1,0:T(8,128)}, u32[]{:S(2)}, u32[]{:S(2)}) collective-permute-start(f32[1024,1024]{1,0:T(8,128)} %maximum_select_fusion.1), channel_id=1, source_target_pairs={{0,16},{16,0},{4,20},{20,4},{8,24},{24,8},{12,28},{28,12},{32,48},... | collective-permute-start | bytes 12582920 | tf_op jit(solution)/shard_map/ppermute | solution.py:27
  813.3 0.9 copy-start.9
  813.4 1.0 copy-start.11
  814.4 4.8 collective-permute-start.21
  814.5 4.7 collective-permute-start.23
  819.1 4.7 collective-permute-start.22
  824.4 4.7 collective-permute-start.24
  829.1 18.8 %collective-permute-start.25 = (f32[384,512]{1,0:T(8,128)S(1)}, f32[384,512]{1,0:T(8,128)S(1)}, u32[]{:S(2)}, u32[]{:S(2)}) collective-permute-start(f32[384,512]{1,0:T(8,128)S(1)} %maximum_select_fusion.8), channel_id=1, source_target_pairs={{0,8},{8,0},{4,12},{12,4},{16,24},{24,16},{20,28},{28,20},{32,40},... | collective-permute-start | bytes 2359304 | tf_op jit(solution)/shard_map/ppermute | solution.py:27
  848.2 70.8 %collective-permute-start.26 = (f32[768,512]{1,0:T(8,128)S(1)}, f32[768,512]{1,0:T(8,128)S(1)}, u32[]{:S(2)}, u32[]{:S(2)}) collective-permute-start(f32[768,512]{1,0:T(8,128)S(1)} %maximum_select_fusion.7), channel_id=1, source_target_pairs={{0,16},{16,0},{4,20},{20,4},{8,24},{24,8},{12,28},{28,12},{32,48},... | collective-permute-start | bytes 4718600 | tf_op jit(solution)/shard_map/ppermute | solution.py:27
  922.3 1.0 copy-start.2
